TPU v7x, 512 devices: a whole 4x4x16 slice. The times are simulated.
512 devices in a mesh: seq: 64 (over x, z), chan: 8 (over y, core).
Axes of the slice: x: 4, y: 4, z: 16, core: 2. Of those that a mesh axis runs over, the one named last changes fastest.
Arguments:
- key_gate: bfloat16 [16384, 8192], P('seq', 'chan'), may hold values from -6 to 6
- values: bfloat16 [16384, 8192], P('seq', 'chan'), may hold values from -6 to 6
- query_gate: bfloat16 [16384, 8192], P('seq', 'chan'), may hold values from -6 to 6
- grad_output: bfloat16 [16384, 8192], P(('seq', 'chan')), may hold values from -6 to 6
- short_taps: bfloat16 [7, 8192], P(None, 'chan'), may hold values from -2 to 2
- long_taps: bfloat16 [128, 8192], P(None, 'chan'), may hold values from -0.5 to 0.5
Outputs:
- grad_query: bfloat16 [16384, 8192], P('seq', 'chan')
- grad_key: bfloat16 [16384, 8192], P('seq', 'chan')
- grad_value: bfloat16 [16384, 8192], P('seq', 'chan')
- grad_long: float32 [128, 8192], P('seq', 'chan')
- grad_short: float32 [7, 8192], P(None, 'chan')
All inputs are finite; a program needn't handle non-finite values.
Results may differ from a plain program's by a relative error of at most 0.0059.
Values may be sent and summed in bfloat16 or wider, within the bound.
A program may use at most 64 MiB of HBM per device.

v0:
```python
import jax
import jax.numpy as jnp
from jax import lax
from jax.sharding import PartitionSpec as P


def passed_along(shard, axis, by):
    length = lax.axis_size(axis)
    pairs = [(i, i + by) for i in range(length) if 0 <= i + by < length]
    return lax.ppermute(shard, axis, pairs)


def depthwise(extended, kernel):
    channels = kernel.shape[2]
    result = lax.conv_general_dilated(
        extended[None],
        kernel,
        (1,),
        [(0, 0)],
        dimension_numbers=("NWC", "WIO", "NWC"),
        feature_group_count=channels,
        preferred_element_type=jnp.float32,
    )
    return result[0]


def causal_apply(extended, weights):
    return depthwise(extended, jnp.flip(weights, 0)[:, None, :])


def forward_apply(extended, weights):
    return depthwise(extended, weights[:, None, :])


def filter_partial(history, grad):
    return jnp.flip(depthwise(history, grad[:, None, :]), 0)


def body(key_gate, values, query_gate, grad_output, short_taps, long_taps):
    long_len = long_taps.shape[0]
    short_len = short_taps.shape[0]
    row_count = key_gate.shape[0]
    cotangent = lax.all_to_all(grad_output, "chan", split_axis=1, concat_axis=0, tiled=True)
    product = (key_gate.astype(jnp.float32) * values.astype(jnp.float32)).astype(jnp.bfloat16)
    grad_mixed = (cotangent.astype(jnp.float32) * query_gate.astype(jnp.float32)).astype(
        jnp.bfloat16
    )
    short_hist = passed_along(product[row_count - (short_len - 1) :], "seq", 1)
    short_ext = jnp.concatenate([short_hist, product], 0)
    short_out = causal_apply(short_ext, short_taps).astype(jnp.bfloat16)
    long_hist = passed_along(short_out[row_count - (long_len - 1) :], "seq", 1)
    long_ext = jnp.concatenate([long_hist, short_out], 0)
    head_long = passed_along(grad_mixed[: long_len - 1], "seq", -1)
    long_back = jnp.concatenate([grad_mixed, head_long], 0)
    grad_conv = forward_apply(long_back, long_taps).astype(jnp.bfloat16)
    head_short = passed_along(grad_conv[: short_len - 1], "seq", -1)
    short_back = jnp.concatenate([grad_conv, head_short], 0)
    mixed = causal_apply(long_ext, long_taps)
    grad_query = (cotangent.astype(jnp.float32) * mixed).astype(jnp.bfloat16)
    grad_product = forward_apply(short_back, short_taps)
    grad_key = (grad_product * values.astype(jnp.float32)).astype(jnp.bfloat16)
    grad_value = (grad_product * key_gate.astype(jnp.float32)).astype(jnp.bfloat16)
    long_part = filter_partial(long_ext, grad_mixed)
    short_part = filter_partial(short_ext, grad_conv)
    grad_long = lax.psum_scatter(long_part, "seq", scatter_dimension=0, tiled=True)
    grad_short = lax.psum(short_part, "seq")
    return (grad_query, grad_key, grad_value, grad_long, grad_short)


def solution(mesh):
    in_specs = (
        P("seq", "chan"),
        P("seq", "chan"),
        P("seq", "chan"),
        P(("seq", "chan"), None),
        P(None, "chan"),
        P(None, "chan"),
    )
    out_specs = (
        P("seq", "chan"),
        P("seq", "chan"),
        P("seq", "chan"),
        P("seq", "chan"),
        P(None, "chan"),
    )
    return jax.shard_map(body, mesh=mesh, in_specs=in_specs, out_specs=out_specs, check_vma=False)
```

profile of v0, /device:TPU:8, one launch (start us, length us, event | category | flops | bytes accessed | tf_op | source)
XLA Modules:
  0.0 632.7 jit_solution(11481029039536911054)
XLA Ops:
  7.2 0.0 all-reduce.3.cloned.1.call-start
  7.2 1.1 copy.87
  8.4 17.2 %all_to_all.13 = bf16[32,8,1024]{2,0,1:T(8,128)(2,1)S(1)} all-to-all(bf16[32,8,1024]{2,0,1:T(8,128)(2,1)S(1)} %bitcast.63), channel_id=1, replica_groups=mesh['seq'=64,'chan'=8] {'chan'}, dimensions={1} | all-to-all | bytes 1048576 | tf_op jit(solution)/shard_map/all_to_all | solution.py:43
  25.5 0.2 fusion.19
  25.7 0.0 copy-start.3
  25.8 1.4 collective-permute-start.2
  27.2 8.3 %collective-permute-done.2 = bf16[127,1024]{1,0:T(8,128)(2,1)S(1)} collective-permute-done((bf16[127,1024]{1,0:T(8,128)(2,1)S(1)}, bf16[127,1024]{1,0:T(8,128)(2,1)S(1)}, u32[]{:S(2)}, u32[]{:S(2)}) %collective-permute-start.2) | collective-permute-done | bytes 260128 | tf_op jit(solution)/shard_map/ppermute | solution.py:10
  35.5 0.1 maximum_bitcast_fusion.1
  35.5 14.2 %fusion.2 = bf16[1,256,1024]{2,0,1:T(2,128)(2,1)S(1)} fusion(bf16[1,383,1024]{2,1,0:T(8,128)(2,1)S(1)} %maximum_bitcast_fusion.1, bf16[128,1,1024]{2,0,1:T(8,128)(2,1)S(1)} %bitcast.65), kind=kOutput, calls=%fused_computation.4 | convolution fusion | flops 67371008 | bytes 1570816 | tf_op jit(solution)/shard_map/conv_general_dilated | solution.py:15
  49.8 1.3 collective-permute-start.3
  51.1 0.2 copy.89
  51.3 4.2 collective-permute-done.3
  55.5 0.0 copy-start.6
  55.5 0.0 copy-start.7
  55.5 0.2 reshape.39
  55.7 0.3 copy.48
  56.1 0.2 copy-done.6
  56.2 0.6 convolution_select_fusion
  56.8 0.6 copy.50
  57.5 0.1 reshape.43
  57.6 0.0 copy-start.4
  57.6 2.6 fusion.14
  60.3 1.8 collective-permute-start
  62.0 0.2 rev.16
  62.3 2.6 rev.17
  64.9 1.3 dynamic-slice
  66.8 0.0 collective-permute-done
  66.8 0.1 maximum_bitcast_fusion.2
  67.0 2.5 fusion.12
  69.6 0.2 rev.19
  69.8 0.2 reshape.32
  70.0 0.3 copy.40
  70.3 0.6 fusion.5
  71.0 0.3 copy.42
  71.3 0.2 reshape.36
  71.5 0.1 slice_bitcast_fusion.2
  71.6 3.8 collective-permute-start.1
  75.4 278.3 %psum.7 = f32[7,1024]{1,0:T(8,128)} all-reduce(f32[7,1024]{1,0:T(8,128)S(1)} %rev.19), channel_id=1, replica_groups=mesh['seq'=64,'chan'=8] {'seq'}, use_global_device_ids=true, to_apply=%region_1.2 | all-reduce | flops 7168 | bytes 57344 | tf_op jit(solution)/shard_map/psum | solution.py:66
  353.8 0.1 maximum_bitcast_fusion
  353.9 13.9 %fusion.8 = f32[1,128,1024]{2,0,1:T(1,128)S(1)} fusion(bf16[1,383,1024]{2,1,0:T(8,128)(2,1)S(1)} %maximum_bitcast_fusion, bf16[256,1,1024]{2,0,1:T(8,128)(2,1)S(1)} %bitcast.60), kind=kOutput, calls=%fused_computation.12 | convolution fusion | flops 67108864 | bytes 1832960 | tf_op jit(solution)/shard_map/conv_general_dilated | solution.py:15
  367.8 0.0 copy-start.5
  367.8 0.1 copy.88
  367.9 2.7 rev.18
  370.6 0.0 all-reduce.3.cloned.1.call-update
  370.6 14.2 %fusion.10 = f32[1,256,1024]{2,0,1:T(1,128)S(1)} fusion(bf16[1,383,1024]{2,1,0:T(8,128)(2,1)S(1)} %maximum_bitcast_fusion, bf16[128,1,1024]{2,0,1:T(8,128)(2,1)S(1)} %bitcast.66), kind=kOutput, calls=%fused_computation.14 | convolution fusion | flops 67108864 | bytes 2095104 | tf_op jit(solution)/shard_map/conv_general_dilated | solution.py:15
  384.8 1.1 fusion.17
  385.9 238.6 %all-reduce.3.cloned.1.call-done = f32[128,1024]{1,0:T(8,128)} async-done(((f32[128,1024]{1,0:T(8,128)}), f32[128,1024]{1,0:T(8,128)}) %all-reduce.3.cloned.1.call-update) | async-done | bytes 524304
  624.4 1.4 constant_dynamic-slice_fusion
  (22 shorter events, 0.3 us)
Async XLA Ops:
  7.2 18.4 %copy-start.2 = (bf16[256,1024]{1,0:T(8,128)(2,1)S(1)}, bf16[256,1024]{1,0:T(8,128)(2,1)}, u32[]{:S(2)}) copy-start(bf16[256,1024]{1,0:T(8,128)(2,1)} %param.8) | copy-start | bytes 1572868
  7.2 617.3 %all-reduce.3.cloned.1.call-start = ((), (), s32[]{:S(2)}) async-start(), calls=%async_computation.1 | async-start | bytes 1048576
  25.7 9.8 %copy-start.3 = (bf16[128,1024]{1,0:T(8,128)(2,1)S(1)}, bf16[128,1024]{1,0:T(8,128)(2,1)}, u32[]{:S(2)}) copy-start(bf16[128,1024]{1,0:T(8,128)(2,1)} %param.11) | copy-start | bytes 786436
  25.8 9.7 %collective-permute-start.2 = (bf16[127,1024]{1,0:T(8,128)(2,1)S(1)}, bf16[127,1024]{1,0:T(8,128)(2,1)S(1)}, u32[]{:S(2)}, u32[]{:S(2)}) collective-permute-start(bf16[127,1024]{1,0:T(8,128)(2,1)S(1)} %slice.33), channel_id=1, source_target_pairs={{8,0},{16,8},{24,16},{32,24},{40,32},{48,40},{56,48},{64,56},{72,6... | collective-permute-start | bytes 780296 | tf_op jit(solution)/shard_map/ppermute | solution.py:10
  49.7 5.7 copy-start
  49.8 5.6 collective-permute-start.3
  55.5 0.7 copy-start.6
  55.5 0.7 copy-start.7
  57.6 4.7 copy-start.4
  60.2 6.7 %copy-start.1 = (bf16[1,256,1024]{2,0,1:T(2,128)(2,1)S(1)}, bf16[1,256,1024]{2,0,1:T(2,128)(2,1)}, u32[]{:S(2)}) copy-start(bf16[1,256,1024]{2,0,1:T(2,128)(2,1)} %copy-done) | copy-start | bytes 1572868
  60.3 6.6 %collective-permute-start = (bf16[6,1024]{1,0:T(8,128)(2,1)S(1)}, bf16[6,1024]{1,0:T(8,128)(2,1)S(1)}, u32[]{:S(2)}, u32[]{:S(2)}) collective-permute-start(bf16[6,1024]{1,0:T(8,128)(2,1)S(1)} %slice.29), channel_id=1, source_target_pairs={{0,8},{8,16},{16,24},{24,32},{32,40},{40,48},{48,56},{56,64},{64,7... | collective-permute-start | bytes 36872 | tf_op jit(solution)/shard_map/ppermute | solution.py:10
  71.6 282.2 %collective-permute-start.1 = (bf16[127,1024]{1,0:T(8,128)(2,1)S(1)}, bf16[127,1024]{1,0:T(8,128)(2,1)S(1)}, u32[]{:S(2)}, u32[]{:S(2)}) collective-permute-start(bf16[127,1024]{1,0:T(8,128)(2,1)S(1)} %slice_bitcast_fusion.2), channel_id=1, source_target_pairs={{0,8},{8,16},{16,24},{24,32},{32,40},{40,48},{48,56},{56,64},{64,7... | collective-permute-start | bytes 780296 | tf_op jit(solution)/shard_map/ppermute | solution.py:10
  367.8 2.8 copy-start.5
Sparse Core Ops, SparseCore 0:
  370.7 253.6 all-reduce.2
where the time goes:
time: 633 us
  blocking collectives  296 us (47%)
  waiting for transfers between devices  251 us (40%)
  matrix products  46 us (7%)
  between operations  15.1 us (2%)
  local copies, waits for them, and re-layouts  12.5 us (2%)
  starting transfers between devices  8.33 us (1%)
    psum x1, blocking collectives, body(): grad_short = lax.psum(short_part, 'seq')  278 us
    unnamed x2, waiting for transfers between devices  239 us
    conv_general_dilated x6, matrix products, depthwise(): lax.conv_general_dilated(extended[None], kernel, (1,), [(0, 0)], dimensio...  46 us
    all_to_all x1, blocking collectives, body(): lax.all_to_all(grad_output, 'chan', split_axis=1, concat_axis=0, tiled=True)  17.2 us
  transfers between devices with their start and end apart: 5, of which 3 were waited for; matrix products, arithmetic and copies ran while one was open for 3% of the time, Pallas kernels for 0%

commit v1 on v0

--- a/solution.py
+++ b/solution.py
@@ -63,7 +63,7 @@
     long_part = filter_partial(long_ext, grad_mixed)
     short_part = filter_partial(short_ext, grad_conv)
     grad_long = lax.psum_scatter(long_part, "seq", scatter_dimension=0, tiled=True)
-    grad_short = lax.psum(short_part, "seq")
+    grad_short = jnp.sum(lax.all_gather(short_part, "seq"), axis=0)
     return (grad_query, grad_key, grad_value, grad_long, grad_short)
 
 

time: 633 us -> 510 us (0.81)
  blocking collectives: 296 us -> 17.2 us
  waiting for transfers between devices: 251 us -> 404 us
    psum x1 -> x0, blocking collectives: 278 us -> none  [body(): grad_short = lax.psum(short_part, 'seq')]
    all_gather x0 -> x1, waiting for transfers between devices: none -> 138 us  [body(): grad_short = jnp.sum(lax.all_gather(short_part, 'seq'), axis=0)]
    unnamed x2 -> x3, waiting for transfers between devices: 239 us -> 248 us
  transfers between devices with their start and end apart: 5 -> 6, of which waited for: 3 -> 6; matrix products, arithmetic and copies ran while one was open for 3% -> 5% of each run, Pallas kernels for 0% -> 0%
where the time goes in v1:
time: 510 us
  waiting for transfers between devices  404 us (79%)
  matrix products  46 us (9%)
  blocking collectives  17.2 us (3%)
  between operations  15.1 us (3%)
  local copies, waits for them, and re-layouts  12.4 us (2%)
  starting transfers between devices  8.83 us (2%)
  other arithmetic  6.55 us (1%)
    unnamed x3, waiting for transfers between devices  248 us
    all_gather x1, waiting for transfers between devices, body(): grad_short = jnp.sum(lax.all_gather(short_part, 'seq'), axis=0)  138 us
    conv_general_dilated x6, matrix products, depthwise(): lax.conv_general_dilated(extended[None], kernel, (1,), [(0, 0)], dimensio...  46 us
    ppermute x4, waiting for transfers between devices, passed_along(): return lax.ppermute(shard, axis, pairs)  17.4 us
    all_to_all x1, blocking collectives, body(): lax.all_to_all(grad_output, 'chan', split_axis=1, concat_axis=0, tiled=True)  17.2 us
  transfers between devices with their start and end apart: 6, of which 6 were waited for; matrix products, arithmetic and copies ran while one was open for 5% of the time, Pallas kernels for 0%

profile of v1, /device:TPU:8, one launch (start us, length us, event | category | flops | bytes accessed | tf_op | source)
XLA Modules:
  0.0 509.9 jit_solution(9885496614068587305)
XLA Ops:
  7.2 0.0 all-reduce.3.cloned.1.call-start
  7.2 1.1 copy.87
  8.4 17.2 %all_to_all.13 = bf16[32,8,1024]{2,0,1:T(8,128)(2,1)S(1)} all-to-all(bf16[32,8,1024]{2,0,1:T(8,128)(2,1)S(1)} %bitcast.64), channel_id=1, replica_groups=mesh['seq'=64,'chan'=8] {'chan'}, dimensions={1} | all-to-all | bytes 1048576 | tf_op jit(solution)/shard_map/all_to_all | solution.py:43
  25.5 0.2 fusion.19
  25.8 1.4 collective-permute-start.2
  27.2 8.3 %collective-permute-done.2 = bf16[127,1024]{1,0:T(8,128)(2,1)S(1)} collective-permute-done((bf16[127,1024]{1,0:T(8,128)(2,1)S(1)}, bf16[127,1024]{1,0:T(8,128)(2,1)S(1)}, u32[]{:S(2)}, u32[]{:S(2)}) %collective-permute-start.2) | collective-permute-done | bytes 260128 | tf_op jit(solution)/shard_map/ppermute | solution.py:10
  35.5 0.1 maximum_bitcast_fusion.1
  35.5 14.2 %fusion.2 = bf16[1,256,1024]{2,0,1:T(2,128)(2,1)S(1)} fusion(bf16[1,383,1024]{2,1,0:T(8,128)(2,1)S(1)} %maximum_bitcast_fusion.1, bf16[128,1,1024]{2,0,1:T(8,128)(2,1)S(1)} %bitcast.66), kind=kOutput, calls=%fused_computation.4 | convolution fusion | flops 67371008 | bytes 1570816 | tf_op jit(solution)/shard_map/conv_general_dilated | solution.py:15
  49.8 1.3 collective-permute-start.3
  51.1 0.2 copy.89
  51.3 4.2 collective-permute-done.3
  55.5 0.0 copy-start.6
  55.5 0.2 reshape.39
  55.7 0.3 copy.48
  56.1 0.2 copy-done.5
  56.2 0.6 convolution_select_fusion
  56.8 0.6 copy.50
  57.5 0.1 reshape.43
  57.6 2.6 fusion.14
  60.2 1.6 collective-permute-start
  61.8 0.2 rev.16
  62.1 1.2 collective-permute-done
  63.3 0.1 maximum_bitcast_fusion.2
  63.4 0.2 reshape.32
  63.6 0.3 copy.40
  64.0 0.6 fusion.5
  64.6 0.3 copy.42
  64.9 0.2 reshape.36
  65.1 0.1 slice_bitcast_fusion.2
  65.2 4.2 collective-permute-start.1
  69.5 3.8 collective-permute-done.1
  73.3 0.1 maximum_bitcast_fusion
  73.4 13.9 %fusion.8 = f32[1,128,1024]{2,0,1:T(1,128)S(1)} fusion(bf16[1,383,1024]{2,1,0:T(8,128)(2,1)S(1)} %maximum_bitcast_fusion, bf16[256,1,1024]{2,0,1:T(8,128)(2,1)S(1)} %bitcast.61), kind=kOutput, calls=%fused_computation.12 | convolution fusion | flops 67108864 | bytes 1832960 | tf_op jit(solution)/shard_map/conv_general_dilated | solution.py:15
  87.3 0.1 copy.88
  87.4 2.6 rev.18
  90.1 0.0 all-reduce.3.cloned.1.call-update
  90.1 0.2 all-gather.4.cloned.1.call-start
  90.3 2.5 fusion.12
  92.9 2.4 rev.19
  95.3 0.0 all-gather.4.cloned.1.call-update
  95.4 0.3 rev.17
  95.7 1.3 dynamic-slice
  97.6 14.2 %fusion.10 = f32[1,256,1024]{2,0,1:T(1,128)S(1)} fusion(bf16[1,383,1024]{2,1,0:T(8,128)(2,1)S(1)} %maximum_bitcast_fusion, bf16[128,1,1024]{2,0,1:T(8,128)(2,1)S(1)} %bitcast.67), kind=kOutput, calls=%fused_computation.14 | convolution fusion | flops 67108864 | bytes 2095104 | tf_op jit(solution)/shard_map/conv_general_dilated | solution.py:15
  111.8 1.1 fusion.17
  112.9 248.4 %all-reduce.3.cloned.1.call-done = f32[128,1024]{1,0:T(8,128)} async-done(((f32[128,1024]{1,0:T(8,128)}), f32[128,1024]{1,0:T(8,128)}) %all-reduce.3.cloned.1.call-update) | async-done | bytes 524304
  361.3 1.4 constant_dynamic-slice_fusion
  362.6 138.0 %all-gather.4.cloned.1.call-done = f32[64,7,1024]{2,1,0:T(8,128)} async-done(((f32[1,7,1024]{2,1,0:T(8,128)}), f32[64,7,1024]{2,1,0:T(8,128)}) %all-gather.4.cloned.1.call-update) | async-done | bytes 1835024 | tf_op jit(solution)/shard_map/all_gather | solution.py:66
  500.6 2.4 reduce_sum.9
  (23 shorter events, 0.3 us)
Async XLA Ops:
  7.2 18.4 %copy-start.2 = (bf16[256,1024]{1,0:T(8,128)(2,1)S(1)}, bf16[256,1024]{1,0:T(8,128)(2,1)}, u32[]{:S(2)}) copy-start(bf16[256,1024]{1,0:T(8,128)(2,1)} %param.8) | copy-start | bytes 1572868
  7.2 354.1 %all-reduce.3.cloned.1.call-start = ((), (), s32[]{:S(2)}) async-start(), calls=%async_computation.2 | async-start | bytes 1048576
  25.7 9.8 %copy-start.3 = (bf16[128,1024]{1,0:T(8,128)(2,1)S(1)}, bf16[128,1024]{1,0:T(8,128)(2,1)}, u32[]{:S(2)}) copy-start(bf16[128,1024]{1,0:T(8,128)(2,1)} %param.11) | copy-start | bytes 786436
  25.8 9.7 %collective-permute-start.2 = (bf16[127,1024]{1,0:T(8,128)(2,1)S(1)}, bf16[127,1024]{1,0:T(8,128)(2,1)S(1)}, u32[]{:S(2)}, u32[]{:S(2)}) collective-permute-start(bf16[127,1024]{1,0:T(8,128)(2,1)S(1)} %slice.33), channel_id=1, source_target_pairs={{8,0},{16,8},{24,16},{32,24},{40,32},{48,40},{56,48},{64,56},{72,6... | collective-permute-start | bytes 780296 | tf_op jit(solution)/shard_map/ppermute | solution.py:10
  49.7 5.7 %copy-start = (bf16[1,256,1024]{2,0,1:T(2,128)(2,1)}, bf16[1,256,1024]{2,0,1:T(2,128)(2,1)S(1)}, u32[]{:S(2)}) copy-start(bf16[1,256,1024]{2,0,1:T(2,128)(2,1)S(1)} %fusion.2) | copy-start | bytes 1572868
  49.8 5.6 %collective-permute-start.3 = (bf16[6,1024]{1,0:T(8,128)(2,1)S(1)}, bf16[6,1024]{1,0:T(8,128)(2,1)S(1)}, u32[]{:S(2)}, u32[]{:S(2)}) collective-permute-start(bf16[6,1024]{1,0:T(8,128)(2,1)S(1)} %bitcast.72), channel_id=1, source_target_pairs={{8,0},{16,8},{24,16},{32,24},{40,32},{48,40},{56,48},{64,56},{72,6... | collective-permute-start | bytes 36872 | tf_op jit(solution)/shard_map/ppermute | solution.py:10
  55.5 0.7 copy-start.5
  55.5 0.7 copy-start.6
  60.2 3.1 collective-permute-start
  65.2 8.1 %collective-permute-start.1 = (bf16[127,1024]{1,0:T(8,128)(2,1)S(1)}, bf16[127,1024]{1,0:T(8,128)(2,1)S(1)}, u32[]{:S(2)}, u32[]{:S(2)}) collective-permute-start(bf16[127,1024]{1,0:T(8,128)(2,1)S(1)} %slice_bitcast_fusion.2), channel_id=1, source_target_pairs={{0,8},{8,16},{16,24},{24,32},{32,40},{40,48},{48,56},{56,64},{64,7... | collective-permute-start | bytes 780296 | tf_op jit(solution)/shard_map/ppermute | solution.py:10
  87.3 3.0 copy-start.1
  90.1 5.3 %copy-start.4 = (bf16[128,1024]{1,0:T(8,128)(2,1)S(1)}, bf16[128,1024]{1,0:T(8,128)(2,1)}, u32[]{:S(2)}) copy-start(bf16[128,1024]{1,0:T(8,128)(2,1)} %param.11) | copy-start | bytes 786436
  90.1 410.5 %all-gather.4.cloned.1.call-start = ((), (), s32[]{:S(2)}) async-start(), calls=%async_computation.1 | async-start | bytes 2129920 | tf_op jit(solution)/shard_map/all_gather | solution.py:66
Sparse Core Ops, SparseCore 0:
  90.2 271.0 all-reduce.2
  365.2 135.3 all-gather.3
